TPU v7x, 32 devices: a whole 2x2x4 slice. The times are simulated.
32 devices in a mesh: seq: 8 (over y, x, core), cb: 4 (over z).
Axes of the slice: x: 2, y: 2, z: 4, core: 2. Of those that a mesh axis runs over, the one named last changes fastest.
Arguments:
- hidden: bfloat16 [2, 1024, 4096], P(None, 'seq'), may hold values from -6 to 6
- temporal_gain: float32 [4096], replicated, may hold values from 0.5 to 2
- temporal_qkv: bfloat16 [3, 4096, 2048], P(None, None, 'cb'), may hold values from -10 to 10
- temporal_out: bfloat16 [2048, 4096], P('cb'), may hold values from -0.125 to 0.125
- codebook_ids: int32 [2, 1024, 4], P(None, 'seq', 'cb'), may hold values from 0 to 2047
- embedding: bfloat16 [4, 2048, 1024], P('cb'), may hold values from -6 to 6
- input_weight: bfloat16 [4, 4096, 1024], P('cb', 'seq'), may hold values from -0.09375 to 0.09375
- depth_gain: float32 [4, 1024], P('cb'), may hold values from 0.5 to 2
- depth_qkv: bfloat16 [4, 3, 1024, 1024], P('cb'), may hold values from -10 to 10
- depth_out: bfloat16 [4, 1024, 1024], P('cb'), may hold values from -0.1875 to 0.1875
Outputs:
- temporal: bfloat16 [2, 1024, 4096], P(None, 'seq')
- depth: bfloat16 [2, 1024, 4, 1024], P(None, 'seq', 'cb')
All inputs are finite; a program needn't handle non-finite values.
Results may differ from a plain program's by a relative error of at most 0.017.
Values may be sent and summed in bfloat16 or wider, within the bound.
No kernel may reach another device: no remote copies, remote signals or barrier semaphores. Data moves between devices by JAX's collectives and lax.ppermute only.
A program may use at most 128 MiB of HBM per device.

v0:
```python
import jax
import jax.numpy as jnp
from jax import lax
from jax.sharding import PartitionSpec as P

HD = 128
DW = 1024
DH = 16
DHD = 64


def normalize(values, scale):
    mean_sq = jnp.mean(values * values, axis=-1, keepdims=True)
    return values * lax.rsqrt(mean_sq + 1e-05) * scale


def shards(
    hidden,
    temporal_gain,
    temporal_qkv,
    temporal_out,
    codebook_ids,
    embedding,
    input_weight,
    depth_gain,
    depth_qkv,
    depth_out,
):
    seq_count, frames, width = hidden.shape
    head_cols = temporal_qkv.shape[2]
    head_count = head_cols // HD
    row_count = seq_count * frames
    hidden_f = hidden.astype(jnp.float32)
    normed = normalize(hidden_f, temporal_gain).astype(jnp.bfloat16).reshape(row_count, width)
    projected = []
    for which in range(3):
        part_rows = jnp.dot(normed, temporal_qkv[which], preferred_element_type=jnp.float32).astype(
            jnp.bfloat16
        )
        projected.append(part_rows.reshape(seq_count, frames, head_count, HD))
    queries = projected[0]
    query_pos = lax.axis_index("seq") * frames + jnp.arange(frames, dtype=jnp.int32)
    temporal_scale = 1.0 / jnp.sqrt(jnp.float32(HD))
    highest = jnp.full((seq_count, head_count, frames), -1e30, jnp.float32)
    key_piece = lax.all_gather(projected[1], "seq", axis=1, tiled=True)
    value_piece = lax.all_gather(projected[2], "seq", axis=1, tiled=True)
    count = key_piece.shape[1]
    scores = (
        jnp.einsum("sqhd,skhd->shqk", queries, key_piece, preferred_element_type=jnp.float32)
        * temporal_scale
    )
    key_pos = jnp.arange(count, dtype=jnp.int32)
    allowed = (key_pos[None, :] <= query_pos[:, None])[None, None]
    scores = jnp.where(allowed, scores, -1e30)
    new_high = jnp.maximum(highest, jnp.max(scores, axis=-1))
    weights = jnp.where(allowed, jnp.exp(scores - new_high[..., None]), 0.0)
    totals = jnp.sum(weights, axis=-1)
    update = jnp.einsum(
        "shqk,skhd->sqhd",
        weights.astype(jnp.bfloat16),
        value_piece,
        preferred_element_type=jnp.float32,
    )
    gathered = update
    highest, totals, gathered = (new_high, totals, gathered)
    mixed = (
        (gathered / totals.transpose(0, 2, 1)[..., None])
        .astype(jnp.bfloat16)
        .reshape(row_count, head_cols)
    )
    term = jnp.dot(mixed, temporal_out, preferred_element_type=jnp.float32)
    summed = lax.psum(term.astype(jnp.bfloat16), "cb").astype(jnp.float32)
    temporal = (hidden_f.reshape(row_count, width) + summed).astype(jnp.bfloat16)
    projected_in = jnp.dot(
        temporal,
        lax.all_gather(input_weight, "seq", axis=1, tiled=True)[0],
        preferred_element_type=jnp.float32,
    )
    entry = jnp.take(embedding[0], codebook_ids.reshape(row_count), axis=0).astype(jnp.float32)
    stream = (projected_in + entry).astype(jnp.bfloat16)
    depth_normed = normalize(stream.astype(jnp.float32), depth_gain[0]).astype(jnp.bfloat16)
    book_query = jnp.dot(depth_normed, depth_qkv[0, 0], preferred_element_type=jnp.float32).astype(
        jnp.bfloat16
    )
    book_key = jnp.dot(depth_normed, depth_qkv[0, 1], preferred_element_type=jnp.float32).astype(
        jnp.bfloat16
    )
    book_value = jnp.dot(depth_normed, depth_qkv[0, 2], preferred_element_type=jnp.float32).astype(
        jnp.bfloat16
    )
    depth_scale = 1.0 / jnp.sqrt(jnp.float32(DHD))
    books = lax.axis_size("cb")
    block_rows = row_count // books
    packed = jnp.concatenate([book_query, book_key, book_value], axis=1).reshape(
        1, books, block_rows, 3 * DW
    )
    arrived = lax.all_to_all(packed, "cb", split_axis=1, concat_axis=0, tiled=True)
    item_count = arrived.shape[2]
    body_rows = arrived.reshape(books, item_count, 3, DH, DHD)
    query_part = body_rows[:, :, 0]
    key_part = body_rows[:, :, 1]
    value_part = body_rows[:, :, 2]
    scores = (
        jnp.einsum("crhd,jrhd->crhj", query_part, key_part, preferred_element_type=jnp.float32)
        * depth_scale
    )
    numbers = jnp.arange(books, dtype=jnp.int32)
    permitted = (numbers[None, :] <= numbers[:, None])[:, None, None, :]
    scores = jnp.where(permitted, scores, -1e30)
    highest_l = jnp.max(scores, axis=-1, keepdims=True)
    weights = jnp.where(permitted, jnp.exp(scores - highest_l), 0.0)
    totals_l = jnp.sum(weights, axis=-1)[..., None]
    result = (
        jnp.einsum(
            "crhj,jrhd->crhd",
            weights.astype(jnp.bfloat16),
            value_part,
            preferred_element_type=jnp.float32,
        )
        / totals_l
    )
    result = result.astype(jnp.bfloat16).reshape(books, 1, item_count, DW)
    returned = lax.all_to_all(result, "cb", split_axis=0, concat_axis=1, tiled=True)
    book_mixed = returned.reshape(row_count, DW)
    depth = (
        jnp.dot(book_mixed, depth_out[0], preferred_element_type=jnp.float32)
        + stream.astype(jnp.float32)
    ).astype(jnp.bfloat16)
    return (temporal.reshape(seq_count, frames, width), depth.reshape(seq_count, frames, 1, DW))


def solution(mesh):
    placed = (
        P(None, "seq", None),
        P(),
        P(None, None, "cb"),
        P("cb", None),
        P(None, "seq", "cb"),
        P("cb", None, None),
        P("cb", "seq", None),
        P("cb", None),
        P("cb", None, None, None),
        P("cb", None, None),
    )
    return jax.shard_map(
        shards,
        mesh=mesh,
        in_specs=placed,
        out_specs=(P(None, "seq", None), P(None, "seq", "cb", None)),
        check_vma=False,
    )
```

profile of v0, /device:TPU:0, one launch (start us, length us, event | category | flops | bytes accessed | tf_op | source)
XLA Modules:
  0.0 334.3 jit_solution(7204706713739142722)
XLA Ops:
  7.2 2.2 multiply_reduce_fusion
  9.5 2.3 multiply_convert_fusion
  11.8 1.3 copy-done.2
  13.1 3.5 %fusion.63 = bf16[256,512]{1,0:T(8,128)(2,1)S(1)} fusion(bf16[256,4096]{1,0:T(8,128)(2,1)S(1)} %bitcast.119, bf16[3,4096,512]{2,1,0:T(8,128)(2,1)} %param.12), kind=kOutput, calls=%fused_computation.54 | convolution fusion | flops 1073872896 | bytes 6553600 | tf_op jit(solution)/shard_map/dot_general | solution.py:37
  16.6 0.1 reshape.148
  16.7 0.8 copy.53
  17.5 0.0 all-gather.4.cloned.1.call-start
  17.5 4.1 %fusion.57 = bf16[256,512]{1,0:T(8,128)(2,1)S(1)} fusion(bf16[256,4096]{1,0:T(8,128)(2,1)} %bitcast.120, bf16[3,4096,512]{2,1,0:T(8,128)(2,1)} %param.12), kind=kOutput, calls=%fused_computation.52 | convolution fusion | flops 1073872896 | bytes 6553600 | tf_op jit(solution)/shard_map/dot_general | solution.py:37
  21.6 0.1 reshape.146
  21.7 0.9 copy.52
  22.6 0.0 all-reduce.2.cloned.1.call-start
  22.6 4.1 %fusion.60 = bf16[256,512]{1,0:T(8,128)(2,1)S(1)} fusion(bf16[256,4096]{1,0:T(8,128)(2,1)} %bitcast.121, bf16[3,4096,512]{2,1,0:T(8,128)(2,1)} %param.12), kind=kOutput, calls=%fused_computation.53 | convolution fusion | flops 1073872896 | bytes 6553600 | tf_op jit(solution)/shard_map/dot_general | solution.py:37
  26.7 0.1 reshape.147
  26.8 0.1 iota_compare_fusion
  26.9 21.2 %all-gather.6.cloned.1.call-done = bf16[2,1024,4,128]{3,1,2,0:T(8,128)(2,1)} async-done(((bf16[2,128,4,128]{3,1,2,0:T(8,128)(2,1)}), bf16[2,1024,4,128]{3,1,2,0:T(8,128)(2,1)}) %all-gather.6.cloned.1.call-update) | async-done | bytes 2097168 | tf_op jit(solution)/shard_map/all_gather | solution.py:45
  48.1 2.6 fusion.12
  50.8 1.9 copy-done.1
  52.7 1.3 fusion.13
  54.0 24.7 %all-gather.4.cloned.1.call-done = bf16[2,1024,4,128]{1,3,2,0:T(8,128)(2,1)} async-done(((bf16[2,128,4,128]{1,3,2,0:T(8,128)(2,1)}), bf16[2,1024,4,128]{1,3,2,0:T(8,128)(2,1)}) %all-gather.4.cloned.1.call-update) | async-done | bytes 2097168 | tf_op jit(solution)/shard_map/all_gather | solution.py:46
  78.7 4.2 %fusion.73 = bf16[2,128,4,128]{1,3,2,0:T(8,128)(2,1)S(1)} fusion(bf16[2,1024,4,128]{1,3,2,0:T(8,128)(2,1)} %all-gather.4.cloned.1.call-done, f32[2,4,128,1024]{3,2,1,0:T(8,128)} %copy-done.1, f32[2,4,128]{2,1,0:T(4,128)S(1)} %broadcast_maximum_fusion, pred[128,1024]{1,0:T(8,128)(4,1)S(1)} %iota_compare_fusion, f32[2,128,4]{1,2,0:T(4,128)S(1)} %bitcast.126), kind=kOutput, calls=%fused_computation.63 | convolution fusion | flops 273940480 | bytes 6692864 | tf_op jit(solution)/shard_map/shqk,skhd->sqhd/dot_general | solution.py:58
  82.9 0.2 copy.55
  83.2 4.8 %convolution_convert_fusion = bf16[256,4096]{1,0:T(8,128)(2,1)} fusion(bf16[512,4096]{1,0:T(8,128)(2,1)} %param.13, bf16[32,8,4,128]{3,2,1,0:T(4,128)(2,1)S(1)} %bitcast.124), kind=kOutput, calls=%fused_computation.3 | convolution fusion | flops 1074790400 | bytes 6553600 | tf_op jit(solution)/shard_map/dot_general | solution.py:71
  87.9 0.2 all-gather.8.cloned.1.call-start
  88.2 0.3 all-gather.8.cloned.1.call-update
  88.6 4.3 %gather_fusion = bf16[256,1024]{1,0:T(8,128)(2,1)S(1)} fusion(bf16[2048,1024]{1,0:T(8,128)(2,1)} %bitcast.117, s32[1024]{0:T(1024)S(1)} %pad_clamp_fusion), kind=kCustom, calls=%fused_computation | custom fusion | bytes 1049600 | tf_op jit(solution)/shard_map/jit(_take)/gather | solution.py:79
  92.9 81.4 %all-reduce.2.cloned.1.call-done = bf16[256,4096]{1,0:T(8,128)(2,1)} async-done(((bf16[256,4096]{1,0:T(8,128)(2,1)}), bf16[256,4096]{1,0:T(8,128)(2,1)}) %all-reduce.2.cloned.1.call-update) | async-done | bytes 2097168 | tf_op jit(solution)/shard_map/psum | solution.py:72
  174.2 4.3 %fusion.8 = bf16[256,4096]{1,0:T(8,128)(2,1)} fusion(bf16[256,4096]{1,0:T(8,128)(2,1)} %all-reduce.2.cloned.1.call-done, bf16[2,128,4096]{2,1,0:T(8,128)(2,1)} %param.10), kind=kLoop, calls=%fused_computation.11 | loop fusion | flops 4194304 | bytes 6291456 | tf_op jit(solution)/shard_map/convert_element_type | solution.py:73
  178.6 50.7 %all-gather.8.cloned.1.call-done = bf16[1,4096,1024]{2,1,0:T(8,128)(2,1)} async-done(((bf16[1,512,1024]{2,1,0:T(8,128)(2,1)}), bf16[1,4096,1024]{2,1,0:T(8,128)(2,1)}) %all-gather.8.cloned.1.call-update) | async-done | bytes 8388624 | tf_op jit(solution)/shard_map/all_gather | solution.py:76
  229.3 6.5 %fusion.66 = (f32[256]{0:T(256)S(1)}, bf16[256,1024]{1,0:T(8,128)(2,1)S(1)}) fusion(bf16[256,1024]{1,0:T(8,128)(2,1)S(1)} %gather_fusion, pred[256]{0:T(512)(128)(4,1)S(1)} %compare_and_fusion, bf16[256,4096]{1,0:T(8,128)(2,1)} %fusion.8, bf16[1,4096,1024]{2,1,0:T(8,128)(2,1)} %all-gather.8.cloned.1.call-done), kind=kOutput, calls=%fused_computation.55 | convolution fusion | flops 2149318400 | bytes 11535616 | tf_op jit(solution)/shard_map/dot_general | solution.py:74
  235.8 2.5 fusion.45
  238.3 2.4 fusion.48
  240.7 2.4 fusion.51
  243.1 1.3 pad_maximum_fusion
  244.3 4.6 %all-to-all-start = ((bf16[1,4,64,3072]{3,2,0,1:T(8,128)(2,1)}), bf16[1,4,64,3072]{3,2,0,1:T(8,128)(2,1)}, u32[]{:S(2)}, u32[]{:S(2)}) async-start(bf16[1,4,64,3072]{3,2,0,1:T(8,128)(2,1)} %bitcast.116), calls=%async_computation | async-start | bytes 3145728 | tf_op jit(solution)/shard_map/all_to_all | solution.py:97
  248.9 37.5 %all-to-all-done = bf16[1,4,64,3072]{3,2,0,1:T(8,128)(2,1)} async-done(((bf16[1,4,64,3072]{3,2,0,1:T(8,128)(2,1)}), bf16[1,4,64,3072]{3,2,0,1:T(8,128)(2,1)}, u32[]{:S(2)}, u32[]{:S(2)}) %all-to-all-start) | async-done | bytes 1572896 | tf_op jit(solution)/shard_map/all_to_all | solution.py:97
  286.4 4.9 %reshape.154 = bf16[4,64,3,16,64]{4,3,2,1,0:T(8,128)(2,1)} reshape(bf16[1,4,64,3072]{3,2,0,1:T(8,128)(2,1)} %all-to-all-done) | data formatting | bytes 3145728 | tf_op jit(solution)/shard_map/reshape | solution.py:99
  291.3 3.5 %fusion.89 = (bf16[4,64,1,16,64]{4,3,2,1,0:T(8,128)(2,1)}, bf16[4,64,1,16,64]{4,3,2,1,0:T(8,128)(2,1)S(1)}, bf16[4,64,1,16,64]{4,3,2,1,0:T(8,128)(2,1)S(1)}) fusion(bf16[4,64,3,16,64]{4,3,2,1,0:T(8,128)(2,1)} %reshape.154), kind=kLoop, calls=%fused_computation.86 | loop fusion | bytes 3145728 | tf_op jit(solution)/shard_map/slice | solution.py:102
  294.8 2.9 fusion.69
  297.7 2.4 copy.60
  300.1 0.1 fusion.80
  300.1 0.1 fusion.81
  300.3 1.8 copy.61
  302.1 1.1 copy.62
  303.2 2.9 fusion.32
  306.0 0.1 copy.63
  306.2 1.5 reshape.155
  307.7 17.5 %all_to_all.8 = bf16[4,1,64,1024]{3,2,1,0:T(8,128)(2,1)S(1)} all-to-all(bf16[4,1,64,1024]{3,2,1,0:T(8,128)(2,1)} %bitcast.122), channel_id=1, replica_groups=mesh['seq'=8,'cb'=4] {'cb'}, dimensions={0} | all-to-all | bytes 1048576 | tf_op jit(solution)/shard_map/all_to_all | solution.py:123
  325.2 2.5 fusion.42
  (22 shorter events, 0.2 us)
Async XLA Ops:
  7.2 318.0 %copy-start = (bf16[1,1024,1024]{2,1,0:T(8,128)(2,1)S(1)}, bf16[1,1024,1024]{2,1,0:T(8,128)(2,1)}, u32[]{:S(2)}) copy-start(bf16[1,1024,1024]{2,1,0:T(8,128)(2,1)} %param.19) | copy-start | bytes 6291460
  7.2 41.0 %all-gather.6.cloned.1.call-start = ((), (), s32[]{:S(2)}) async-start(), calls=%async_computation.3 | async-start | bytes 2359296 | tf_op jit(solution)/shard_map/all_gather | solution.py:45
  11.8 1.3 copy-start.2
  17.5 61.2 %all-gather.4.cloned.1.call-start = ((), (), s32[]{:S(2)}) async-start(), calls=%async_computation.2 | async-start | bytes 2359296 | tf_op jit(solution)/shard_map/all_gather | solution.py:46
  22.6 151.7 %all-reduce.2.cloned.1.call-start = ((), (), s32[]{:S(2)}) async-start(), calls=%async_computation.4 | async-start | bytes 4194304 | tf_op jit(solution)/shard_map/psum | solution.py:72
  50.8 1.9 copy-start.1
  83.1 5.4 %copy-start.3 = (s32[2,128,1]{1,2,0:T(1,128)S(1)}, s32[2,128,1]{1,2,0:T(1,128)}, u32[]{:S(2)}) copy-start(s32[2,128,1]{1,2,0:T(1,128)} %param.14) | copy-start | bytes 3076
  87.9 141.4 %all-gather.8.cloned.1.call-start = ((), (), s32[]{:S(2)}) async-start(), calls=%async_computation.5 | async-start | bytes 9437184 | tf_op jit(solution)/shard_map/all_gather | solution.py:76
  178.6 57.2 %copy-start.4 = (f32[1,1024]{1,0:T(1,128)S(1)}, f32[1,1024]{1,0:T(1,128)}, u32[]{:S(2)}) copy-start(f32[1,1024]{1,0:T(1,128)} %param.17) | copy-start | bytes 12292
  235.8 4.9 %copy-start.5 = (bf16[256,1024]{1,0:T(8,128)(2,1)}, bf16[256,1024]{1,0:T(8,128)(2,1)S(1)}, u32[]{:S(2)}) copy-start(bf16[256,1024]{1,0:T(8,128)(2,1)S(1)} %get-tuple-element.20) | copy-start | bytes 1572868
  244.3 42.1 %all-to-all-start = ((bf16[1,4,64,3072]{3,2,0,1:T(8,128)(2,1)}), bf16[1,4,64,3072]{3,2,0,1:T(8,128)(2,1)}, u32[]{:S(2)}, u32[]{:S(2)}) async-start(bf16[1,4,64,3072]{3,2,0,1:T(8,128)(2,1)} %bitcast.116), calls=%async_computation | async-start | bytes 3145728 | tf_op jit(solution)/shard_map/all_to_all | solution.py:97
Sparse Core Ops, SparseCore 0:
  17.6 30.4 all-gather.5
  50.6 28.0 all-gather.3
  88.1 86.1 all-reduce.1
  176.0 53.2 all-gather.7
where the time goes:
time: 335 us; the launch traced here: 334 us
  waiting for transfers between devices  216 us (64%)
  matrix products  45.2 us (13%)
  local copies, waits for them, and re-layouts  24.8 us (7%)
  blocking collectives  17.5 us (5%)
  between operations  14 us (4%)
  other arithmetic  11.9 us (4%)
  starting transfers between devices  4.93 us (1%)
    psum x1, waiting for transfers between devices, shards(): summed = lax.psum(term.astype(jnp.bfloat16), 'cb').astype(jnp.float32)  81.4 us
    all_gather x1, waiting for transfers between devices, shards(): lax.all_gather(input_weight, 'seq', axis=1, tiled=True)[0]  50.7 us
    all_to_all x1, waiting for transfers between devices, shards(): lax.all_to_all(packed, 'cb', split_axis=1, concat_axis=0, tiled=True)  37.5 us
    all_gather x1, waiting for transfers between devices, shards(): value_piece = lax.all_gather(projected[2], 'seq', axis=1, tiled=True)  24.7 us
    all_gather x1, waiting for transfers between devices, shards(): key_piece = lax.all_gather(projected[1], 'seq', axis=1, tiled=True)  21.2 us
    all_to_all x1, blocking collectives, shards(): lax.all_to_all(result, 'cb', split_axis=0, concat_axis=1, tiled=True)  17.5 us
    dot_general x3, matrix products, shards(): jnp.dot(normed, temporal_qkv[which], preferred_element_type=jnp.float32)  11.6 us
  transfers between devices with their start and end apart: 5, of which 5 were waited for; matrix products, arithmetic and copies ran while one was open for 7% of the time, Pallas kernels for 0%

commit v1 on v0

--- a/solution.py
+++ b/solution.py
@@ -94,7 +94,10 @@
     packed = jnp.concatenate([book_query, book_key, book_value], axis=1).reshape(
         1, books, block_rows, 3 * DW
     )
-    arrived = lax.all_to_all(packed, "cb", split_axis=1, concat_axis=0, tiled=True)
+    arrived = jnp.concatenate(
+        lax.all_to_all(jnp.stack(jnp.split(packed, lax.axis_size("cb"), axis=1)), "cb", 0, 0),
+        axis=0,
+    )
     item_count = arrived.shape[2]
     body_rows = arrived.reshape(books, item_count, 3, DH, DHD)
     query_part = body_rows[:, :, 0]

time: 335 us -> 334 us (level)
    another operation x0 -> x2, local copies, waits for them, and re-layouts: none -> 4.97 us  [the longest x1 4.87 us: shards(): body_rows = arrived.reshape(books, item_count, 3, DH, DHD)]
    reshape x1 -> x0, local copies, waits for them, and re-layouts: 4.87 us -> none  [shards(): body_rows = arrived.reshape(books, item_count, 3, DH, DHD)]
where the time goes in v1:
time: 334 us
  waiting for transfers between devices  216 us (65%)
  matrix products  45.2 us (14%)
  local copies, waits for them, and re-layouts  25 us (7%)
  blocking collectives  17.5 us (5%)
  between operations  14 us (4%)
  other arithmetic  11.1 us (3%)
  starting transfers between devices  4.96 us (1%)
    psum x1, waiting for transfers between devices, shards(): summed = lax.psum(term.astype(jnp.bfloat16), 'cb').astype(jnp.float32)  81.3 us
    all_gather x1, waiting for transfers between devices, shards(): lax.all_gather(input_weight, 'seq', axis=1, tiled=True)[0]  50.7 us
    all_to_all x1, waiting for transfers between devices, shards(): lax.all_to_all(jnp.stack(jnp.split(packed, lax.axis_size('cb'), axis=1)),...  37.5 us
    all_gather x1, waiting for transfers between devices, shards(): value_piece = lax.all_gather(projected[2], 'seq', axis=1, tiled=True)  24.7 us
    all_gather x1, waiting for transfers between devices, shards(): key_piece = lax.all_gather(projected[1], 'seq', axis=1, tiled=True)  21.2 us
    all_to_all x1, blocking collectives, shards(): lax.all_to_all(result, 'cb', split_axis=0, concat_axis=1, tiled=True)  17.5 us
    dot_general x3, matrix products, shards(): jnp.dot(normed, temporal_qkv[which], preferred_element_type=jnp.float32)  11.6 us
  transfers between devices with their start and end apart: 5, of which 5 were waited for; matrix products, arithmetic and copies ran while one was open for 7% of the time, Pallas kernels for 0%

profile of v1, /device:TPU:0, one launch (start us, length us, event | category | flops | bytes accessed | tf_op | source)
XLA Modules:
  0.0 333.7 jit_solution(13559045948277048717)
XLA Ops:
  7.2 2.2 multiply_reduce_fusion
  9.5 0.1 copy-done.1
  9.6 1.3 multiply_convert_fusion
  11.0 1.3 copy-done.3
  12.3 3.5 %fusion.63 = bf16[256,512]{1,0:T(8,128)(2,1)S(1)} fusion(bf16[256,4096]{1,0:T(8,128)(2,1)S(1)} %bitcast.123, bf16[3,4096,512]{2,1,0:T(8,128)(2,1)} %param.12), kind=kOutput, calls=%fused_computation.55 | convolution fusion | flops 1073872896 | bytes 6553600 | tf_op jit(solution)/shard_map/dot_general | solution.py:37
  15.8 0.7 copy.54
  16.6 4.1 %fusion.57 = bf16[256,512]{1,0:T(8,128)(2,1)S(1)} fusion(bf16[256,4096]{1,0:T(8,128)(2,1)} %bitcast.124, bf16[3,4096,512]{2,1,0:T(8,128)(2,1)} %param.12), kind=kOutput, calls=%fused_computation.53 | convolution fusion | flops 1073872896 | bytes 6553600 | tf_op jit(solution)/shard_map/dot_general | solution.py:37
  20.7 0.1 reshape.139
  20.8 0.9 copy.53
  21.7 4.1 %fusion.60 = bf16[256,512]{1,0:T(8,128)(2,1)S(1)} fusion(bf16[256,4096]{1,0:T(8,128)(2,1)} %bitcast.125, bf16[3,4096,512]{2,1,0:T(8,128)(2,1)} %param.12), kind=kOutput, calls=%fused_computation.54 | convolution fusion | flops 1073872896 | bytes 6553600 | tf_op jit(solution)/shard_map/dot_general | solution.py:37
  25.9 0.1 iota_compare_fusion
  26.0 21.2 %all-gather.6.cloned.1.call-done = bf16[2,1024,4,128]{3,1,2,0:T(8,128)(2,1)} async-done(((bf16[2,128,4,128]{3,1,2,0:T(8,128)(2,1)}), bf16[2,1024,4,128]{3,1,2,0:T(8,128)(2,1)}) %all-gather.6.cloned.1.call-update) | async-done | bytes 2097168 | tf_op jit(solution)/shard_map/all_gather | solution.py:45
  47.3 2.6 fusion.12
  49.9 1.9 copy-done.2
  51.8 1.3 fusion.13
  53.2 24.7 %all-gather.4.cloned.1.call-done = bf16[2,1024,4,128]{1,3,2,0:T(8,128)(2,1)} async-done(((bf16[2,128,4,128]{1,3,2,0:T(8,128)(2,1)}), bf16[2,1024,4,128]{1,3,2,0:T(8,128)(2,1)}) %all-gather.4.cloned.1.call-update) | async-done | bytes 2097168 | tf_op jit(solution)/shard_map/all_gather | solution.py:46
  77.8 4.2 %fusion.73 = bf16[2,128,4,128]{1,3,2,0:T(8,128)(2,1)S(1)} fusion(bf16[2,1024,4,128]{1,3,2,0:T(8,128)(2,1)} %all-gather.4.cloned.1.call-done, f32[2,4,128,1024]{3,2,1,0:T(8,128)} %copy-done.2, f32[2,4,128]{2,1,0:T(4,128)S(1)} %broadcast_maximum_fusion, pred[128,1024]{1,0:T(8,128)(4,1)S(1)} %iota_compare_fusion, f32[2,128,4]{1,2,0:T(4,128)S(1)} %bitcast.130), kind=kOutput, calls=%fused_computation.64 | convolution fusion | flops 273940480 | bytes 6692864 | tf_op jit(solution)/shard_map/shqk,skhd->sqhd/dot_general | solution.py:58
  82.1 0.2 copy.56
  82.3 4.8 %convolution_convert_fusion = bf16[256,4096]{1,0:T(8,128)(2,1)} fusion(bf16[512,4096]{1,0:T(8,128)(2,1)} %param.13, bf16[32,8,4,128]{3,2,1,0:T(4,128)(2,1)S(1)} %bitcast.128), kind=kOutput, calls=%fused_computation.3 | convolution fusion | flops 1074790400 | bytes 6553600 | tf_op jit(solution)/shard_map/dot_general | solution.py:71
  87.0 0.2 all-gather.8.cloned.1.call-start
  87.3 0.3 all-gather.8.cloned.1.call-update
  87.6 0.1 copy-done.4
  87.7 4.3 %gather_fusion = bf16[256,1024]{1,0:T(8,128)(2,1)S(1)} fusion(bf16[2048,1024]{1,0:T(8,128)(2,1)} %bitcast.121, s32[1024]{0:T(1024)S(1)} %pad_clamp_fusion), kind=kCustom, calls=%fused_computation | custom fusion | bytes 1049600 | tf_op jit(solution)/shard_map/jit(_take)/gather | solution.py:79
  92.0 81.3 %all-reduce.2.cloned.1.call-done = bf16[256,4096]{1,0:T(8,128)(2,1)} async-done(((bf16[256,4096]{1,0:T(8,128)(2,1)}), bf16[256,4096]{1,0:T(8,128)(2,1)}) %all-reduce.2.cloned.1.call-update) | async-done | bytes 2097168 | tf_op jit(solution)/shard_map/psum | solution.py:72
  173.3 4.3 %fusion.8 = bf16[256,4096]{1,0:T(8,128)(2,1)} fusion(bf16[256,4096]{1,0:T(8,128)(2,1)} %all-reduce.2.cloned.1.call-done, bf16[2,128,4096]{2,1,0:T(8,128)(2,1)} %param.10), kind=kLoop, calls=%fused_computation.11 | loop fusion | flops 4194304 | bytes 6291456 | tf_op jit(solution)/shard_map/convert_element_type | solution.py:73
  177.7 50.7 %all-gather.8.cloned.1.call-done = bf16[1,4096,1024]{2,1,0:T(8,128)(2,1)} async-done(((bf16[1,512,1024]{2,1,0:T(8,128)(2,1)}), bf16[1,4096,1024]{2,1,0:T(8,128)(2,1)}) %all-gather.8.cloned.1.call-update) | async-done | bytes 8388624 | tf_op jit(solution)/shard_map/all_gather | solution.py:76
  228.4 6.5 %fusion.66 = (f32[256]{0:T(256)S(1)}, bf16[256,1024]{1,0:T(8,128)(2,1)S(1)}) fusion(bf16[256,1024]{1,0:T(8,128)(2,1)S(1)} %gather_fusion, pred[256]{0:T(512)(128)(4,1)S(1)} %compare_and_fusion, bf16[256,4096]{1,0:T(8,128)(2,1)} %fusion.8, bf16[1,4096,1024]{2,1,0:T(8,128)(2,1)} %all-gather.8.cloned.1.call-done), kind=kOutput, calls=%fused_computation.56 | convolution fusion | flops 2149318400 | bytes 11535616 | tf_op jit(solution)/shard_map/dot_general | solution.py:74
  234.9 2.5 fusion.45
  237.4 2.4 fusion.48
  239.8 2.4 fusion.51
  242.2 0.1 pad_maximum_fusion
  242.3 0.1 slice_bitcast_fusion.3
  242.4 1.4 pad_maximum_fusion.1
  243.8 4.6 %all-to-all-start = ((bf16[4,1,1,64,3072]{4,3,2,1,0:T(8,128)(2,1)}), bf16[4,1,1,64,3072]{4,3,2,1,0:T(8,128)(2,1)}, u32[]{:S(2)}, u32[]{:S(2)}) async-start(bf16[4,1,1,64,3072]{4,3,2,1,0:T(8,128)(2,1)} %pad_maximum_fusion.1), calls=%async_computation | async-start | bytes 3145728 | tf_op jit(solution)/shard_map/all_to_all | solution.py:98
  248.4 37.5 %all-to-all-done = bf16[4,1,1,64,3072]{4,3,2,1,0:T(8,128)(2,1)} async-done(((bf16[4,1,1,64,3072]{4,3,2,1,0:T(8,128)(2,1)}), bf16[4,1,1,64,3072]{4,3,2,1,0:T(8,128)(2,1)}, u32[]{:S(2)}, u32[]{:S(2)}) %all-to-all-start) | async-done | bytes 1572896 | tf_op jit(solution)/shard_map/all_to_all | solution.py:98
  285.8 4.9 %reshape_reshape.3 = bf16[4,64,3,16,64]{4,3,2,1,0:T(8,128)(2,1)} reshape(bf16[4,1,1,64,3072]{4,3,2,1,0:T(8,128)(2,1)} %all-to-all-done) | data formatting | bytes 3145728 | tf_op jit(solution)/shard_map/reshape;reshape | solution.py:102
  290.7 3.5 %fusion.89 = (bf16[4,64,1,16,64]{4,3,2,1,0:T(8,128)(2,1)}, bf16[4,64,1,16,64]{4,3,2,1,0:T(8,128)(2,1)S(1)}, bf16[4,64,1,16,64]{4,3,2,1,0:T(8,128)(2,1)S(1)}) fusion(bf16[4,64,3,16,64]{4,3,2,1,0:T(8,128)(2,1)} %reshape_reshape.3), kind=kLoop, calls=%fused_computation.91 | loop fusion | bytes 3145728 | tf_op jit(solution)/shard_map/slice | solution.py:105
  294.2 2.9 fusion.69
  297.1 2.4 copy.60
  299.5 0.1 fusion.80
  299.6 0.1 fusion.81
  299.7 1.8 copy.61
  301.5 1.1 copy.62
  302.6 2.9 fusion.32
  305.4 0.1 copy.63
  305.6 1.5 reshape.147
  307.1 17.5 %all_to_all.14 = bf16[4,1,64,1024]{3,2,1,0:T(8,128)(2,1)S(1)} all-to-all(bf16[4,1,64,1024]{3,2,1,0:T(8,128)(2,1)} %bitcast.126), channel_id=1, replica_groups=mesh['seq'=8,'cb'=4] {'cb'}, dimensions={0} | all-to-all | bytes 1048576 | tf_op jit(solution)/shard_map/all_to_all | solution.py:126
  324.6 2.5 fusion.42
  (26 shorter events, 0.4 us)
Async XLA Ops:
  7.2 317.4 %copy-start = (bf16[1,1024,1024]{2,1,0:T(8,128)(2,1)S(1)}, bf16[1,1024,1024]{2,1,0:T(8,128)(2,1)}, u32[]{:S(2)}) copy-start(bf16[1,1024,1024]{2,1,0:T(8,128)(2,1)} %param.19) | copy-start | bytes 6291460
  7.2 40.1 %all-gather.6.cloned.1.call-start = ((), (), s32[]{:S(2)}) async-start(), calls=%async_computation.3 | async-start | bytes 2359296 | tf_op jit(solution)/shard_map/all_gather | solution.py:45
  7.2 2.4 copy-start.1
  10.9 1.3 copy-start.3
  16.6 61.2 %all-gather.4.cloned.1.call-start = ((), (), s32[]{:S(2)}) async-start(), calls=%async_computation.2 | async-start | bytes 2359296 | tf_op jit(solution)/shard_map/all_gather | solution.py:46
  21.7 151.7 %all-reduce.2.cloned.1.call-start = ((), (), s32[]{:S(2)}) async-start(), calls=%async_computation.4 | async-start | bytes 4194304 | tf_op jit(solution)/shard_map/psum | solution.py:72
  49.9 1.9 copy-start.2
  87.0 0.7 copy-start.4
  87.0 141.4 %all-gather.8.cloned.1.call-start = ((), (), s32[]{:S(2)}) async-start(), calls=%async_computation.5 | async-start | bytes 9437184 | tf_op jit(solution)/shard_map/all_gather | solution.py:76
  177.7 57.2 %copy-start.5 = (f32[1,1024]{1,0:T(1,128)S(1)}, f32[1,1024]{1,0:T(1,128)}, u32[]{:S(2)}) copy-start(f32[1,1024]{1,0:T(1,128)} %param.17) | copy-start | bytes 12292
  234.9 4.9 %copy-start.6 = (bf16[256,1024]{1,0:T(8,128)(2,1)}, bf16[256,1024]{1,0:T(8,128)(2,1)S(1)}, u32[]{:S(2)}) copy-start(bf16[256,1024]{1,0:T(8,128)(2,1)S(1)} %get-tuple-element.24) | copy-start | bytes 1572868
  243.8 42.1 %all-to-all-start = ((bf16[4,1,1,64,3072]{4,3,2,1,0:T(8,128)(2,1)}), bf16[4,1,1,64,3072]{4,3,2,1,0:T(8,128)(2,1)}, u32[]{:S(2)}, u32[]{:S(2)}) async-start(bf16[4,1,1,64,3072]{4,3,2,1,0:T(8,128)(2,1)} %pad_maximum_fusion.1), calls=%async_computation | async-start | bytes 3145728 | tf_op jit(solution)/shard_map/all_to_all | solution.py:98
Sparse Core Ops, SparseCore 0:
  16.7 30.4 all-gather.5
  49.7 28.0 all-gather.3
  87.2 86.1 all-reduce.1
  175.1 53.2 all-gather.7
